TPU v7x, 32 devices: a whole 2x2x4 slice. The times are simulated.
32 devices in a mesh: dp: 8 (over z, x), mp: 4 (over y, core).
Axes of the slice: x: 2, y: 2, z: 4, core: 2. Of those that a mesh axis runs over, the one named last changes fastest.
Arguments:
- images: bfloat16 [128, 196, 512], P('dp'), may hold values from -6 to 6
- cotangent: bfloat16 [128, 196, 512], P('dp'), may hold values from -6 to 6
- qkv_weight: float32 [1536, 512], P(('mp', 'dp')), may hold values from -0.25 to 0.25
- proj_weight: float32 [512, 512], P(('mp', 'dp')), may hold values from -0.5 to 0.5
- expand_weight: float32 [2048, 512], P(('mp', 'dp')), may hold values from -0.25 to 0.25
- contract_weight: float32 [2048, 512], P(('mp', 'dp')), may hold values from -0.125 to 0.125
- qkv_moment: float32 [1536, 512], P(('mp', 'dp')), may hold values from -256 to 256
- proj_moment: float32 [512, 512], P(('mp', 'dp')), may hold values from -256 to 256
- expand_moment: float32 [2048, 512], P(('mp', 'dp')), may hold values from -192 to 192
- contract_moment: float32 [2048, 512], P(('mp', 'dp')), may hold values from -384 to 384
- vectors: float32 [6, 512], replicated, may hold values from -1.2 to 2.2
- qv_bias: float32 [2, 512], P(None, 'mp'), may hold values from -3 to 3
- expand_bias: float32 [2048], P('mp'), may hold values from -3 to 3
- rel_table: float32 [169, 16], P(None, 'mp'), may hold values from -3 to 334
- vectors_first: float32 [6, 512], replicated, may hold values from -80 to 80
- vectors_second: float32 [6, 512], replicated, may hold values from 7.5264 to 30.1056
- qv_first: float32 [2, 512], P(None, 'mp'), may hold values from -40 to 40
- qv_second: float32 [2, 512], P(None, 'mp'), may hold values from 2.5088 to 10.0352
- expand_bias_first: float32 [2048], P('mp'), may hold values from -20 to 20
- expand_bias_second: float32 [2048], P('mp'), may hold values from 0.75264 to 2.5088
- table_first: float32 [169, 16], P(None, 'mp'), may hold values from -6 to 6
- table_second: float32 [169, 16], P(None, 'mp'), may hold values from 0.0075264 to 0.0301056
- region_ids: int32 [14, 14], replicated, may hold values from 0 to 3
- pos_index: int32 [49, 49], replicated, may hold values from 0 to 168
- image_counts: int32 [8], P('dp'), may hold values from 1 to 16, as said below
Outputs:
- block_out: bfloat16 [128, 196, 512], P('dp')
- input_grad: bfloat16 [128, 196, 512], P('dp')
- qkv_grad: float32 [1536, 512], P(('mp', 'dp'))
- proj_grad: float32 [512, 512], P(('mp', 'dp'))
- expand_grad: float32 [2048, 512], P(('mp', 'dp'))
- contract_grad: float32 [2048, 512], P(('mp', 'dp'))
- vectors_grad: float32 [6, 512], replicated
- qv_grad: float32 [2, 512], P(None, 'mp')
- expand_bias_grad: float32 [2048], P('mp')
- table_grad: float32 [169, 16], P(None, 'mp')
- qkv_step: float32 [1536, 512], P(('mp', 'dp'))
- proj_step: float32 [512, 512], P(('mp', 'dp'))
- expand_step: float32 [2048, 512], P(('mp', 'dp'))
- contract_step: float32 [2048, 512], P(('mp', 'dp'))
- qkv_moment_new: float32 [1536, 512], P(('mp', 'dp'))
- proj_moment_new: float32 [512, 512], P(('mp', 'dp'))
- expand_moment_new: float32 [2048, 512], P(('mp', 'dp'))
- contract_moment_new: float32 [2048, 512], P(('mp', 'dp'))
- vectors_step: float32 [6, 512], replicated
- qv_step: float32 [2, 512], P(None, 'mp')
- expand_bias_step: float32 [2048], P('mp')
- table_step: float32 [169, 16], P(None, 'mp')
- vectors_first_new: float32 [6, 512], replicated
- vectors_second_new: float32 [6, 512], replicated
- qv_first_new: float32 [2, 512], P(None, 'mp')
- qv_second_new: float32 [2, 512], P(None, 'mp')
- expand_bias_first_new: float32 [2048], P('mp')
- expand_bias_second_new: float32 [2048], P('mp')
- table_first_new: float32 [169, 16], P(None, 'mp')
- table_second_new: float32 [169, 16], P(None, 'mp')
Inputs may be any that keep to these rules, and one draw needn't show every extreme that they name: `image_counts`: some index of dp has all 16 images live.
All inputs are finite; a program needn't handle non-finite values.
Results may differ from a plain program's by a relative error of at most 0.018.
The roundings to bfloat16 on the way count: a program that leaves them out, or rounds other values in their place, can miss the bound.
Values may be sent and summed in bfloat16 or wider, within the bound.
A program may use at most 192 MiB of HBM per device.

v0:
```python
import math

import jax
import jax.numpy as jnp
from jax import lax
from jax.sharding import PartitionSpec as P

C = 512
HD = 32
FF = 2048
WIN = 7
SIDE = 14
SHIFT = 3
NS_ITERS = 5
MB = 2
IMG_DEV = 16
TABLE = 169


norm_eps = 1e-05
ns_eps = 1e-07
coef_a = 3.4445
coef_b = -4.775
coef_c = 2.0315
muon_rate = 0.3
muon_decay = 0.1
muon_beta = 0.95
adam_rate = 0.1
adam_one = 0.9
adam_two = 0.999
adam_eps = 1e-08
adam_step = 4
mask_value = -100.0
highest = lax.Precision.HIGHEST
contract_rows = (((0,), (0,)), ((), ()))
contract_cols = (((1,), (1,)), ((), ()))


def to_windows(field_values):
    image_total = field_values.shape[0]
    channels = field_values.shape[-1]
    blocks = SIDE // WIN
    grid_values = field_values.reshape(image_total, SIDE, SIDE, channels)
    grid_values = jnp.roll(grid_values, (-SHIFT, -SHIFT), axis=(1, 2))
    grid_values = grid_values.reshape(image_total, blocks, WIN, blocks, WIN, channels)
    grid_values = grid_values.transpose(0, 1, 3, 2, 4, 5)
    return grid_values.reshape(image_total * blocks * blocks, WIN * WIN, channels)


def from_windows(window_values, image_total):
    channels = window_values.shape[-1]
    blocks = SIDE // WIN
    grid_values = window_values.reshape(image_total, blocks, blocks, WIN, WIN, channels)
    grid_values = grid_values.transpose(0, 1, 3, 2, 4, 5).reshape(image_total, SIDE, SIDE, channels)
    grid_values = jnp.roll(grid_values, (SHIFT, SHIFT), axis=(1, 2))
    return grid_values.reshape(image_total, SIDE * SIDE, channels)


def normalize(values):
    mean_value = jnp.mean(values, axis=-1, keepdims=True)
    centered = values - mean_value
    variance = jnp.mean(centered * centered, axis=-1, keepdims=True)
    inv_scale = lax.rsqrt(variance + norm_eps)
    return (centered * inv_scale, inv_scale)


def normalize_back(grad_norm, normed, inv_scale, gain):
    scaled = grad_norm * gain
    return inv_scale * (
        scaled
        - jnp.mean(scaled, axis=-1, keepdims=True)
        - normed * jnp.mean(scaled * normed, axis=-1, keepdims=True)
    )


def gelu_value(values):
    return 0.5 * values * (1.0 + lax.erf(values * (1.0 / math.sqrt(2.0))))


def gelu_slope(values):
    return 0.5 * (1.0 + lax.erf(values * (1.0 / math.sqrt(2.0)))) + values * jnp.exp(
        -0.5 * values * values
    ) * (1.0 / math.sqrt(2.0 * math.pi))


def gram_of(matrix):
    return jnp.dot(matrix.T, matrix, precision=highest)


def poly_step(matrix, gram):
    poly = coef_b * gram + coef_c * jnp.dot(gram, gram, precision=highest)
    return coef_a * matrix + jnp.dot(matrix, poly, precision=highest)


def orthogonalize_shared(blocks):
    iterates = list(blocks)
    for iteration in range(NS_ITERS):
        grams = lax.psum(
            (
                gram_of(iterates[0]),
                gram_of(iterates[1]),
                gram_of(iterates[2]),
                gram_of(iterates[3]),
            ),
            ("dp", "mp"),
        )
        grams = list(grams)
        if iteration == 0:
            norm_values = [jnp.sqrt(jnp.trace(gram)) + ns_eps for gram in grams]
            iterates = [matrix / norm_value for matrix, norm_value in zip(iterates, norm_values)]
            grams = [
                gram / (norm_value * norm_value) for gram, norm_value in zip(grams, norm_values)
            ]
        iterates = [poly_step(matrix, gram) for matrix, gram in zip(iterates, grams)]
    return tuple(iterates)


def adam_update(grad_sum, first_moment, second_moment):
    first_new = adam_one * first_moment + (1.0 - adam_one) * grad_sum
    second_new = adam_two * second_moment + (1.0 - adam_two) * grad_sum * grad_sum
    first_hat = first_new / (1.0 - adam_one**adam_step)
    second_hat = second_new / (1.0 - adam_two**adam_step)
    return (-adam_rate * first_hat / (jnp.sqrt(second_hat) + adam_eps), first_new, second_new)


def layer_pass(
    image_block,
    cot_block,
    live_block,
    gathered,
    vectors,
    qv_bias,
    expand_bias,
    pos_bias,
    window_mask,
    onehot,
):
    qkv_local, proj_local, expand_local, contract_local = gathered
    image_total = image_block.shape[0]
    heads_here = pos_bias.shape[0]
    wide = heads_here * HD
    span = WIN * WIN
    window_count = image_total * (SIDE // WIN) ** 2
    token_count = image_total * SIDE * SIDE
    score_scale = 1.0 / math.sqrt(HD)
    tokens_in = image_block.astype(jnp.float32)
    normed_one, inv_one = normalize(tokens_in)
    first_in = (normed_one * vectors[0] + vectors[1]).astype(jnp.bfloat16)
    window_in = to_windows(first_in).reshape(window_count * span, C)
    zero_bias = jnp.zeros((heads_here, HD), jnp.float32)
    joint_bias = jnp.stack(
        [qv_bias[0].reshape(heads_here, HD), zero_bias, qv_bias[1].reshape(heads_here, HD)], axis=1
    ).reshape(3 * wide)
    projected_qkv = lax.dot_general(
        window_in, qkv_local, contract_cols, preferred_element_type=jnp.float32
    )
    qkv_low = (
        (projected_qkv + joint_bias)
        .astype(jnp.bfloat16)
        .reshape(window_count, span, heads_here, 3, HD)
    )
    queries = qkv_low[:, :, :, 0]
    keys_part = qkv_low[:, :, :, 1]
    values_part = qkv_low[:, :, :, 2]

    def score_block():
        raw_scores = (
            jnp.einsum("wihd,wjhd->whij", queries, keys_part, preferred_element_type=jnp.float32)
            * score_scale
        )
        raw_scores = raw_scores.reshape(
            image_total, window_count // image_total, heads_here, span, span
        )
        raw_scores = raw_scores + pos_bias[None, None] + window_mask[None, :, None]
        return raw_scores.reshape(window_count, heads_here, span, span)

    scores = score_block()
    row_top = jnp.max(scores, axis=-1, keepdims=True)
    exponent = jnp.exp(scores - row_top)
    row_total = jnp.sum(exponent, axis=-1, keepdims=True)
    attention = exponent / row_total
    log_total = row_top + jnp.log(row_total)
    attended = jnp.einsum(
        "whij,wjhd->wihd",
        attention.astype(jnp.bfloat16),
        values_part,
        preferred_element_type=jnp.float32,
    )
    attended = attended.astype(jnp.bfloat16).reshape(window_count * span, wide)
    proj_part = jnp.dot(attended, proj_local, preferred_element_type=jnp.float32)
    projected = lax.psum(proj_part, "mp")
    middle = tokens_in + (
        from_windows(projected.reshape(window_count, span, C), image_total) + vectors[4]
    )
    normed_two, inv_two = normalize(middle)
    second_in = (normed_two * vectors[2] + vectors[3]).astype(jnp.bfloat16).reshape(token_count, C)
    hidden = (
        lax.dot_general(second_in, expand_local, contract_cols, preferred_element_type=jnp.float32)
        + expand_bias
    )
    acted = gelu_value(hidden).astype(jnp.bfloat16)
    mlp_part = jnp.dot(acted, contract_local, preferred_element_type=jnp.float32)
    mlp_out = lax.psum(mlp_part.astype(jnp.bfloat16), "mp").astype(jnp.float32)
    block_out = middle + (mlp_out.reshape(image_total, SIDE * SIDE, C) + vectors[5])
    block_low = jnp.where(live_block[:, None, None], block_out, 0.0).astype(jnp.bfloat16)
    grad_out = cot_block.astype(jnp.float32) * live_block.astype(jnp.float32)[:, None, None]
    out_low = grad_out.astype(jnp.bfloat16).reshape(token_count, C)
    contract_grad = lax.dot_general(
        acted, out_low, contract_rows, preferred_element_type=jnp.float32
    )
    acted_grad = lax.dot_general(
        out_low, contract_local, contract_cols, preferred_element_type=jnp.float32
    )
    hidden_grad = (acted_grad * gelu_slope(hidden)).astype(jnp.bfloat16)
    expand_bias_grad = jnp.sum(hidden_grad.astype(jnp.float32), axis=0)
    expand_grad = lax.dot_general(
        hidden_grad, second_in, contract_rows, preferred_element_type=jnp.float32
    )
    second_part = jnp.dot(hidden_grad, expand_local, preferred_element_type=jnp.float32)
    second_grad = lax.psum(second_part, "mp").reshape(image_total, SIDE * SIDE, C)
    middle_grad = grad_out + normalize_back(second_grad, normed_two, inv_two, vectors[2])
    attn_low = to_windows(middle_grad.astype(jnp.bfloat16)).reshape(window_count * span, C)
    proj_grad = lax.dot_general(
        attended, attn_low, contract_rows, preferred_element_type=jnp.float32
    )
    attended_grad = lax.dot_general(
        attn_low, proj_local, contract_cols, preferred_element_type=jnp.float32
    )
    attended_grad = attended_grad.astype(jnp.bfloat16).reshape(window_count, span, heads_here, HD)
    attention_again = jnp.exp(score_block() - log_total)
    value_grad = jnp.einsum(
        "whij,wihd->wjhd",
        attention_again.astype(jnp.bfloat16),
        attended_grad,
        preferred_element_type=jnp.float32,
    )
    probs_grad = jnp.einsum(
        "wihd,wjhd->whij", attended_grad, values_part, preferred_element_type=jnp.float32
    )
    row_term = jnp.sum(attention_again * probs_grad, axis=-1, keepdims=True)
    score_grad = (attention_again * (probs_grad - row_term)).astype(jnp.bfloat16)
    query_grad = (
        jnp.einsum("whij,wjhd->wihd", score_grad, keys_part, preferred_element_type=jnp.float32)
        * score_scale
    )
    key_grad = (
        jnp.einsum("whij,wihd->wjhd", score_grad, queries, preferred_element_type=jnp.float32)
        * score_scale
    )
    bias_heads = (
        jnp.sum(score_grad.astype(jnp.float32), axis=0)
        .transpose(1, 2, 0)
        .reshape(span * span, heads_here)
    )
    table_grad = jnp.dot(onehot.T, bias_heads, precision=highest)
    qkv_back = (
        jnp.stack([query_grad, key_grad, value_grad], axis=3)
        .astype(jnp.bfloat16)
        .reshape(window_count * span, 3 * wide)
    )
    kind_sums = jnp.sum(qkv_back.astype(jnp.float32), axis=0).reshape(heads_here, 3, HD)
    qv_grad = jnp.stack([kind_sums[:, 0].reshape(wide), kind_sums[:, 2].reshape(wide)], axis=0)
    qkv_grad = lax.dot_general(
        qkv_back, window_in, contract_rows, preferred_element_type=jnp.float32
    )
    first_part = jnp.dot(qkv_back, qkv_local, preferred_element_type=jnp.float32)
    first_windows = lax.psum(first_part.astype(jnp.bfloat16), "mp").astype(jnp.float32)
    first_grad = from_windows(first_windows.reshape(window_count, span, C), image_total)
    input_grad = middle_grad + normalize_back(first_grad, normed_one, inv_one, vectors[0])
    vectors_grad = jnp.stack(
        [
            jnp.sum(first_grad * normed_one, axis=(0, 1)),
            jnp.sum(first_grad, axis=(0, 1)),
            jnp.sum(second_grad * normed_two, axis=(0, 1)),
            jnp.sum(second_grad, axis=(0, 1)),
            jnp.sum(middle_grad, axis=(0, 1)),
            jnp.sum(grad_out, axis=(0, 1)),
        ],
        axis=0,
    )
    big_grads = (qkv_grad, proj_grad, expand_grad, contract_grad)
    small_grads = (vectors_grad, qv_grad, expand_bias_grad, table_grad)
    return (block_low, input_grad.astype(jnp.bfloat16), big_grads, small_grads)


def shards(
    images,
    cotangent,
    qkv_weight,
    proj_weight,
    expand_weight,
    contract_weight,
    qkv_moment,
    proj_moment,
    expand_moment,
    contract_moment,
    vectors,
    qv_bias,
    expand_bias,
    rel_table,
    vectors_first,
    vectors_second,
    qv_first,
    qv_second,
    expand_bias_first,
    expand_bias_second,
    table_first,
    table_second,
    region_ids,
    pos_index,
    image_counts,
):
    span = WIN * WIN
    live_all = jnp.arange(IMG_DEV, dtype=jnp.int32) < image_counts[0]
    onehot = (
        pos_index.reshape(span * span)[:, None] == jnp.arange(TABLE, dtype=jnp.int32)[None, :]
    ).astype(jnp.float32)
    heads_here = rel_table.shape[1]
    pos_bias = (
        jnp.dot(onehot, rel_table, precision=highest)
        .reshape(span, span, heads_here)
        .transpose(2, 0, 1)
    )
    window_regions = to_windows(region_ids.reshape(1, SIDE * SIDE, 1))[:, :, 0]
    window_mask = jnp.where(
        window_regions[:, :, None] != window_regions[:, None, :], mask_value, 0.0
    ).astype(jnp.float32)
    qkv_shard_low = qkv_weight.astype(jnp.bfloat16)
    proj_shard_low = proj_weight.astype(jnp.bfloat16)
    expand_shard_low = expand_weight.astype(jnp.bfloat16)
    contract_shard_low = contract_weight.astype(jnp.bfloat16)
    per_batch = IMG_DEV // MB
    out_blocks = []
    input_blocks = []
    for batch_index in range(MB):
        first_image = batch_index * per_batch
        gathered = (
            lax.all_gather(qkv_shard_low, "dp", axis=0, tiled=True),
            lax.all_gather(proj_shard_low, "dp", axis=0, tiled=True),
            lax.all_gather(expand_shard_low, "dp", axis=0, tiled=True),
            lax.all_gather(contract_shard_low, "dp", axis=0, tiled=True),
        )
        block_low, input_low, big_local, small_local = layer_pass(
            images[first_image : first_image + per_batch],
            cotangent[first_image : first_image + per_batch],
            live_all[first_image : first_image + per_batch],
            gathered,
            vectors,
            qv_bias,
            expand_bias,
            pos_bias,
            window_mask,
            onehot,
        )
        out_blocks.append(block_low)
        input_blocks.append(input_low)
        if batch_index == 0:
            big_totals = big_local
            small_totals = small_local
        else:
            big_totals = jax.tree.map(jnp.add, big_totals, big_local)
            small_totals = jax.tree.map(jnp.add, small_totals, small_local)
    shares = (
        lax.psum_scatter(big_totals[0], "dp", scatter_dimension=0, tiled=True),
        lax.psum_scatter(big_totals[1], "dp", scatter_dimension=0, tiled=True),
        lax.psum_scatter(big_totals[2], "dp", scatter_dimension=0, tiled=True),
        lax.psum_scatter(big_totals[3], "dp", scatter_dimension=0, tiled=True),
    )
    small_sums = lax.psum(
        (small_totals[0], small_totals[1], small_totals[2], small_totals[3]), "dp"
    )
    weights_all = (qkv_weight, proj_weight, expand_weight, contract_weight)
    moments = (qkv_moment, proj_moment, expand_moment, contract_moment)
    buffers = tuple(
        (muon_beta * moment + grad_share for moment, grad_share in zip(moments, shares))
    )
    nesterov = tuple(
        (grad_share + muon_beta * buffer_new for grad_share, buffer_new in zip(shares, buffers))
    )
    ortho = orthogonalize_shared(nesterov)
    factors = (math.sqrt(3.0), 1.0, math.sqrt(max(1.0, FF / C)), 1.0)
    new_steps = tuple(
        (
            -muon_rate * (muon_decay * weight + factor * ortho_part)
            for weight, ortho_part, factor in zip(weights_all, ortho, factors)
        )
    )
    vectors_step, vectors_first_new, vectors_second_new = adam_update(
        small_sums[0], vectors_first, vectors_second
    )
    qv_step, qv_first_new, qv_second_new = adam_update(small_sums[1], qv_first, qv_second)
    expand_bias_step, expand_bias_first_new, expand_bias_second_new = adam_update(
        small_sums[2], expand_bias_first, expand_bias_second
    )
    table_step, table_first_new, table_second_new = adam_update(
        small_sums[3], table_first, table_second
    )
    block_out = jnp.concatenate(out_blocks, axis=0)
    input_grad = jnp.concatenate(input_blocks, axis=0)
    return (
        block_out,
        input_grad,
        shares[0],
        shares[1],
        shares[2],
        shares[3],
        small_sums[0],
        small_sums[1],
        small_sums[2],
        small_sums[3],
        new_steps[0],
        new_steps[1],
        new_steps[2],
        new_steps[3],
        buffers[0],
        buffers[1],
        buffers[2],
        buffers[3],
        vectors_step,
        qv_step,
        expand_bias_step,
        table_step,
        vectors_first_new,
        vectors_second_new,
        qv_first_new,
        qv_second_new,
        expand_bias_first_new,
        expand_bias_second_new,
        table_first_new,
        table_second_new,
    )


def solution(mesh):
    return jax.shard_map(
        shards,
        mesh=mesh,
        in_specs=(
            P("dp", None, None),
            P("dp", None, None),
            P(("mp", "dp"), None),
            P(("mp", "dp"), None),
            P(("mp", "dp"), None),
            P(("mp", "dp"), None),
            P(("mp", "dp"), None),
            P(("mp", "dp"), None),
            P(("mp", "dp"), None),
            P(("mp", "dp"), None),
            P(),
            P(None, "mp"),
            P("mp"),
            P(None, "mp"),
            P(),
            P(),
            P(None, "mp"),
            P(None, "mp"),
            P("mp"),
            P("mp"),
            P(None, "mp"),
            P(None, "mp"),
            P(),
            P(),
            P("dp"),
        ),
        out_specs=(
            P("dp", None, None),
            P("dp", None, None),
            P(("mp", "dp"), None),
            P(("mp", "dp"), None),
            P(("mp", "dp"), None),
            P(("mp", "dp"), None),
            P(),
            P(None, "mp"),
            P("mp"),
            P(None, "mp"),
            P(("mp", "dp"), None),
            P(("mp", "dp"), None),
            P(("mp", "dp"), None),
            P(("mp", "dp"), None),
            P(("mp", "dp"), None),
            P(("mp", "dp"), None),
            P(("mp", "dp"), None),
            P(("mp", "dp"), None),
            P(),
            P(None, "mp"),
            P("mp"),
            P(None, "mp"),
            P(),
            P(),
            P(None, "mp"),
            P(None, "mp"),
            P("mp"),
            P("mp"),
            P(None, "mp"),
            P(None, "mp"),
        ),
        check_vma=False,
    )
```

profile of v0, /device:TPU:1, one launch (start us, length us, event | category | flops | bytes accessed | tf_op | source)
XLA Modules:
  0.0 1668.3 jit_solution(11063937340789518265)
XLA Ops:
  21.1 25.6 %all_gather.17 = bf16[128,512]{1,0:T(8,128)(2,1)S(1)} all-gather(bf16[16,512]{1,0:T(8,128)(2,1)S(1)} %convert_element_type.194), channel_id=1, replica_groups=mesh['dp'=8,'mp'=4] {'dp'}, dimensions={0}, use_global_device_ids=true | all-gather | bytes 147456 | tf_op jit(solution)/shard_map/all_gather | solution.py:339
  46.6 27.7 %all_gather.16 = bf16[384,512]{1,0:T(8,128)(2,1)} all-gather(bf16[48,512]{1,0:T(8,128)(2,1)S(1)} %convert_element_type.189), channel_id=1, replica_groups=mesh['dp'=8,'mp'=4] {'dp'}, dimensions={0}, use_global_device_ids=true | all-gather | bytes 442368 | tf_op jit(solution)/shard_map/all_gather | solution.py:338
  88.4 10.3 reshape.374
  100.4 10.5 reshape.385
  118.3 3.8 reshape.386
  134.6 6.6 copy.239
  144.0 6.6 copy.249
  153.1 2.9 fusion.42
  161.3 27.4 %all_gather.19 = bf16[512,512]{1,0:T(8,128)(2,1)} all-gather(bf16[64,512]{1,0:T(8,128)(2,1)S(1)} %convert_element_type.198), channel_id=1, replica_groups=mesh['dp'=8,'mp'=4] {'dp'}, dimensions={0}, use_global_device_ids=true | all-gather | bytes 589824 | tf_op jit(solution)/shard_map/all_gather | solution.py:341
  188.6 26.9 %all_gather.18 = bf16[512,512]{1,0:T(8,128)(2,1)} all-gather(bf16[64,512]{1,0:T(8,128)(2,1)S(1)} %convert_element_type.196), channel_id=1, replica_groups=mesh['dp'=8,'mp'=4] {'dp'}, dimensions={0}, use_global_device_ids=true | all-gather | bytes 589824 | tf_op jit(solution)/shard_map/all_gather | solution.py:340
  215.5 69.2 %all-reduce.30.cloned.1.call-done = (f32[8,14,14,512]{3,0,2,1:T(8,128)}, f32[8,14,14,512]{3,0,2,1:T(8,128)}) async-done(((f32[8,14,14,512]{3,0,2,1:T(8,128)}, f32[8,14,14,512]{3,0,2,1:T(8,128)}), (f32[8,14,14,512]{3,0,2,1:T(8,128)}, f32[8,14,14,512]{3,0,2,1:T(8,128)})) %all-reduce.30.cloned.1.call-update) | async-done | bytes 6422544 | tf_op jit(solution)/shard_map/psum | solution.py:191
  307.9 3.1 copy.240
  313.4 4.2 multiply_convert_fusion.3
  322.8 4.5 multiply_convert_fusion.2
  333.8 3.2 fusion.176
  342.9 3.0 fusion.175
  348.2 107.6 %all-reduce.28.cloned.1.call-done = (f32[1568,512]{1,0:T(8,128)}, f32[1568,512]{1,0:T(8,128)}) async-done(((f32[1568,512]{1,0:T(8,128)}, f32[1568,512]{1,0:T(8,128)}), (f32[1568,512]{1,0:T(8,128)}, f32[1568,512]{1,0:T(8,128)})) %all-reduce.28.cloned.1.call-update) | async-done | bytes 6422544 | tf_op jit(solution)/shard_map/psum | solution.py:220
  455.9 3.7 reshape.393
  459.6 4.2 fusion.149
  463.8 3.4 reshape.401
  475.5 12.5 multiply_reduce_fusion.2
  488.2 6.6 fusion.155
  501.6 3.7 reshape_reshape.36
  508.1 3.4 reshape.411
  511.6 3.8 copy.272
  515.4 4.6 fusion.66
  529.6 3.7 reshape_reshape.34
  536.1 3.4 reshape.410
  539.5 3.6 copy.257
  543.1 3.1 convert_reduce_fusion
  546.2 3.7 copy.277
  549.9 7.0 convert_element_type.232
  556.9 4.5 multiply_reduce_fusion.1
  568.9 3.7 copy.262
  572.6 6.6 convert_element_type.220
  591.6 3.0 fusion.130
  594.6 3.0 fusion.131
  597.6 57.0 %reduce-scatter.7.cloned.1.call-done = f32[16,512]{1,0:T(8,128)} async-done(((f32[128,512]{1,0:T(8,128)}), f32[16,512]{1,0:T(8,128)}) %reduce-scatter.7.cloned.1.call-update) | async-done | bytes 32784 | tf_op jit(solution)/shard_map/reduce_scatter | solution.py:365
  658.3 62.6 %reduce-scatter.5.cloned.1.call-done = f32[48,512]{1,0:T(8,128)} async-done(((f32[384,512]{1,0:T(8,128)}), f32[48,512]{1,0:T(8,128)}) %reduce-scatter.5.cloned.1.call-update) | async-done | bytes 98320 | tf_op jit(solution)/shard_map/reduce_scatter | solution.py:364
  722.5 3.0 fusion.133
  725.7 144.0 %all-reduce.26.cloned.1.call-done = (f32[512,512]{1,0:T(8,128)}, f32[512,512]{1,0:T(8,128)}, f32[512,512]{1,0:T(8,128)}, f32[512,512]{1,0:T(8,128)}) async-done(((f32[512,512]{1,0:T(8,128)}, f32[512,512]{1,0:T(8,128)}, f32[512,512]{1,0:T(8,128)}, f32[512,512]{1,0:T(8,128)}), (f32[512,512]{1,0:T(8,128)}, f32[512,512]{1,0:T(8,128)}, f32[512,512]{1,0:T(8,128)}, ...) | async-done | bytes 4194320 | tf_op jit(solution)/shard_map/psum | solution.py:98
  880.1 4.1 fusion.96
  901.5 3.7 convolution_convert_fusion.3
  907.7 3.7 copy.241
  916.0 3.3 copy.251
  922.1 3.7 reshape_reshape.37
  925.7 3.8 copy.278
  931.8 3.7 reshape_reshape.35
  935.4 3.7 copy.263
  939.6 104.6 %all-reduce.24.cloned.1.call-done = (f32[512,512]{1,0:T(8,128)}, f32[512,512]{1,0:T(8,128)}, f32[512,512]{1,0:T(8,128)}, f32[512,512]{1,0:T(8,128)}) async-done(((f32[512,512]{1,0:T(8,128)}, f32[512,512]{1,0:T(8,128)}, f32[512,512]{1,0:T(8,128)}, f32[512,512]{1,0:T(8,128)}), (f32[512,512]{1,0:T(8,128)}, f32[512,512]{1,0:T(8,128)}, f32[512,512]{1,0:T(8,128)}, ...) | async-done | bytes 4194320 | tf_op jit(solution)/shard_map/psum | solution.py:98
  1044.2 3.9 fusion.90
  1075.1 94.0 %all-reduce.32.cloned.1.call-done = (bf16[8,14,14,512]{3,0,2,1:T(8,128)(2,1)}, bf16[8,14,14,512]{3,0,2,1:T(8,128)(2,1)}, bf16[8,196,512]{2,0,1:T(8,128)(2,1)}, bf16[8,196,512]{2,0,1:T(8,128)(2,1)}) async-done(((bf16[8,14,14,512]{3,0,2,1:T(8,128)(2,1)}, bf16[8,14,14,512]{3,0,2,1:T(8,128)(2,1)}, bf16[8,196,512]{2,0,1:T(8,128)(2,1)}, bf16[8,196,512]{2,0,1:T(8,128)(2,1)}), (bf16[8,14,14,512]{3,0,2,1:T(8,128)(2,1)}, ...) | async-done | bytes 6422544 | tf_op jit(solution)/shard_map/psum | solution.py:267
  1175.1 4.0 multiply_reduce_fusion.7
  1182.4 135.2 %all-reduce.22.cloned.1.call-done = (f32[512,512]{1,0:T(8,128)}, f32[512,512]{1,0:T(8,128)}, f32[512,512]{1,0:T(8,128)}, f32[512,512]{1,0:T(8,128)}) async-done(((f32[512,512]{1,0:T(8,128)}, f32[512,512]{1,0:T(8,128)}, f32[512,512]{1,0:T(8,128)}, f32[512,512]{1,0:T(8,128)}), (f32[512,512]{1,0:T(8,128)}, f32[512,512]{1,0:T(8,128)}, f32[512,512]{1,0:T(8,128)}, ...) | async-done | bytes 4194320 | tf_op jit(solution)/shard_map/psum | solution.py:98
  1317.6 4.2 fusion.94
  1341.2 8.8 fusion.30
  1351.2 2.9 select_convert_fusion.1
  1354.2 128.0 %all-reduce.20.cloned.1.call-done = (f32[512,512]{1,0:T(8,128)}, f32[512,512]{1,0:T(8,128)}, f32[512,512]{1,0:T(8,128)}, f32[512,512]{1,0:T(8,128)}) async-done(((f32[512,512]{1,0:T(8,128)}, f32[512,512]{1,0:T(8,128)}, f32[512,512]{1,0:T(8,128)}, f32[512,512]{1,0:T(8,128)}), (f32[512,512]{1,0:T(8,128)}, f32[512,512]{1,0:T(8,128)}, f32[512,512]{1,0:T(8,128)}, ...) | async-done | bytes 4194320 | tf_op jit(solution)/shard_map/psum | solution.py:98
  1482.2 4.2 fusion.93
  1503.3 4.2 pad_maximum_fusion.4
  1522.3 30.0 %all-reduce.5 = (f32[6,512]{1,0:T(8,128)}, f32[2,128]{1,0:T(2,128)}, f32[512]{0:T(512)}, f32[169,4]{0,1:T(4,128)S(1)}) all-reduce(f32[6,512]{1,0:T(8,128)} %add.597, f32[2,128]{1,0:T(2,128)} %maximum_add_fusion, f32[512]{0:T(512)} %add.599, f32[169,4]{0,1:T(4,128)} %fusion.114), channel_id=1, replica_groups=mesh['dp'=8,'mp'=4] {'dp'}, use_global_device_ids=true, to_apply=%region_48.49 | all-reduce | flops 4516 | bytes 36128 | tf_op jit(solution)/shard_map/psum | solution.py:369
  1552.3 6.6 fusion.29
  1563.6 82.5 %all-reduce.18.cloned.1.call-done = (f32[512,512]{1,0:T(8,128)}, f32[512,512]{1,0:T(8,128)}, f32[512,512]{1,0:T(8,128)}, f32[512,512]{1,0:T(8,128)}) async-done(((f32[512,512]{1,0:T(8,128)}, f32[512,512]{1,0:T(8,128)}, f32[512,512]{1,0:T(8,128)}, f32[512,512]{1,0:T(8,128)}), (f32[512,512]{1,0:T(8,128)}, f32[512,512]{1,0:T(8,128)}, f32[512,512]{1,0:T(8,128)}, ...) | async-done | bytes 4194320 | tf_op jit(solution)/shard_map/psum | solution.py:98
  1646.1 3.9 fusion.92
  (592 shorter events, 300.5 us)
Async XLA Ops:
  7.2 11.6 copy-start
  7.2 277.5 %all-reduce.30.cloned.1.call-start = ((), (), s32[]{:S(2)}) async-start(), calls=%async_computation.14 | async-start | bytes 12845056 | tf_op jit(solution)/shard_map/psum | solution.py:191
  7.3 5.8 copy-start.5
  134.6 6.6 copy-start.54
  150.6 305.3 %all-reduce.28.cloned.1.call-start = ((), (), s32[]{:S(2)}) async-start(), calls=%async_computation.13 | async-start | bytes 12845056 | tf_op jit(solution)/shard_map/psum | solution.py:220
  333.8 254.9 %reduce-scatter.11.cloned.1.call-start = ((), (), s32[]{:S(2)}) async-start(), calls=%async_computation.7 | async-start | bytes 1179648 | tf_op jit(solution)/shard_map/reduce_scatter | solution.py:367
  339.3 250.6 %reduce-scatter.9.cloned.1.call-start = ((), (), s32[]{:S(2)}) async-start(), calls=%async_computation.6 | async-start | bytes 1179648 | tf_op jit(solution)/shard_map/reduce_scatter | solution.py:366
  339.3 6.6 copy-start.21
  339.4 6.6 copy-start.37
  348.2 306.5 %reduce-scatter.7.cloned.1.call-start = ((), (), s32[]{:S(2)}) async-start(), calls=%async_computation.5 | async-start | bytes 294912 | tf_op jit(solution)/shard_map/reduce_scatter | solution.py:365
  475.5 12.6 copy-start.3
  475.5 12.6 copy-start.12
  475.5 12.7 copy-start.13
  475.5 12.7 copy-start.17
  475.5 12.7 copy-start.71
  475.5 12.7 copy-start.73
  475.5 12.7 copy-start.118
  475.5 12.7 copy-start.119
  475.5 12.7 copy-start.145
  475.5 12.7 copy-start.147
  505.4 10.0 copy-start.97
  549.9 7.0 copy-start.96
  583.9 137.0 %reduce-scatter.5.cloned.1.call-start = ((), (), s32[]{:S(2)}) async-start(), calls=%async_computation.4 | async-start | bytes 884736 | tf_op jit(solution)/shard_map/reduce_scatter | solution.py:364
  588.6 66.1 %copy-start.135 = (f32[16,512]{1,0:T(8,128)S(1)}, f32[16,512]{1,0:T(8,128)}, u32[]{:S(2)}) copy-start(f32[16,512]{1,0:T(8,128)} %param.32) | copy-start | bytes 98308
  588.6 281.2 %all-reduce.26.cloned.1.call-start = ((), (), s32[]{:S(2)}) async-start(), calls=%async_computation.12 | async-start | bytes 8388608 | tf_op jit(solution)/shard_map/psum | solution.py:98
  589.6 300.6 %copy-start.93 = (f32[64,512]{1,0:T(8,128)}, f32[64,512]{1,0:T(8,128)S(1)}, u32[]{:S(2)}) copy-start(f32[64,512]{1,0:T(8,128)S(1)} %multiply_add_fusion.3) | copy-start | bytes 393220
  655.4 240.4 %copy-start.126 = (f32[16,512]{1,0:T(8,128)}, f32[16,512]{1,0:T(8,128)S(1)}, u32[]{:S(2)}) copy-start(f32[16,512]{1,0:T(8,128)S(1)} %multiply_add_fusion.15) | copy-start | bytes 98308
  725.5 318.7 %all-reduce.24.cloned.1.call-start = ((), (), s32[]{:S(2)}) async-start(), calls=%async_computation.11 | async-start | bytes 8388608 | tf_op jit(solution)/shard_map/psum | solution.py:98
  891.0 8.2 copy-start.62
  891.0 7.5 copy-start.101
  891.0 7.5 copy-start.103
  901.5 267.7 %all-reduce.32.cloned.1.call-start = ((), (), s32[]{:S(2)}) async-start(), calls=%async_computation.15 | async-start | bytes 12845056 | tf_op jit(solution)/shard_map/psum | solution.py:267
  913.5 5.8 copy-start.153
  913.5 5.8 copy-start.154
  939.1 378.5 %all-reduce.22.cloned.1.call-start = ((), (), s32[]{:S(2)}) async-start(), calls=%async_computation.10 | async-start | bytes 8388608 | tf_op jit(solution)/shard_map/psum | solution.py:98
  1044.2 6.6 copy-start.47
  1048.7 6.7 copy-start.106
  1048.7 6.7 copy-start.46
  1053.4 6.7 copy-start.45
  1062.8 9.2 copy-start.142
  1064.8 417.4 %all-reduce.20.cloned.1.call-start = ((), (), s32[]{:S(2)}) async-start(), calls=%async_computation.9 | async-start | bytes 8388608 | tf_op jit(solution)/shard_map/psum | solution.py:98
  1317.6 7.0 copy-start.44
  1322.5 6.5 copy-start.42
  1327.1 7.1 copy-start.110
  1327.1 7.1 copy-start.40
  1339.6 306.5 %all-reduce.18.cloned.1.call-start = ((), (), s32[]{:S(2)}) async-start(), calls=%async_computation.8 | async-start | bytes 8388608 | tf_op jit(solution)/shard_map/psum | solution.py:98
  1341.1 10.1 copy-start.4
  1341.1 10.1 copy-start.80
  1341.1 10.1 copy-start.81
  1341.1 10.1 copy-start.143
  1341.1 10.1 copy-start.151
  1341.1 10.1 copy-start.152
  1354.2 132.2 %copy-start.85 = (f32[48,512]{1,0:T(8,128)S(1)}, f32[48,512]{1,0:T(8,128)}, u32[]{:S(2)}) copy-start(f32[48,512]{1,0:T(8,128)} %copy-done.84) | copy-start | bytes 294916
  1482.2 7.0 copy-start.50
  1487.2 6.6 copy-start.49
  1491.7 6.7 copy-start.108
  1491.7 6.7 copy-start.48
  1503.3 49.0 %copy-start.7 = (bf16[16,196,512]{2,0,1:T(8,128)(2,1)S(1)}, bf16[16,196,512]{2,0,1:T(8,128)(2,1)}, u32[]{:S(2)}) copy-start(bf16[16,196,512]{2,0,1:T(8,128)(2,1)} %param.25) | copy-start | bytes 9633796
  1552.3 10.0 copy-start.150
  1561.2 88.9 %copy-start.87 = (f32[48,512]{1,0:T(8,128)S(1)}, f32[48,512]{1,0:T(8,128)}, u32[]{:S(2)}) copy-start(f32[48,512]{1,0:T(8,128)} %copy-done.86) | copy-start | bytes 294916
  1561.2 88.9 %copy-start.124 = (f32[48,512]{1,0:T(8,128)S(1)}, f32[48,512]{1,0:T(8,128)}, u32[]{:S(2)}) copy-start(f32[48,512]{1,0:T(8,128)} %param.27) | copy-start | bytes 294916
  1646.1 7.2 copy-start.109
  1646.1 7.2 copy-start.132
  1654.6 6.7 copy-start.1
  (111 other events, 347.1 us)
Sparse Core Ops, SparseCore 0:
  150.7 133.9 all-reduce.29
  333.9 121.9 all-reduce.27
  459.9 62.9 reduce-scatter.10
  526.7 63.1 reduce-scatter.8
  593.7 60.9 reduce-scatter.6
  658.4 62.4 reduce-scatter.4
  727.3 142.3 all-reduce.25
  901.6 142.5 all-reduce.23
  1046.7 122.3 all-reduce.31
  1175.4 142.1 all-reduce.21
  1339.7 142.4 all-reduce.19
  1503.4 142.6 all-reduce.17
where the time goes:
time: 1680 us; the launch traced here: 1670 us
  waiting for transfers between devices  985 us (59%)
  local copies, waits for them, and re-layouts  202 us (12%)
  matrix products  201 us (12%)
  blocking collectives  138 us (8%)
  other arithmetic  121 us (7%)
  between operations  20.3 us (1%)
    psum x5, waiting for transfers between devices, orthogonalize_shared(): lax.psum((gram_of(iterates[0]), gram_of(iterates[1]), gram_of(iterates[2]...  594 us
    psum x1, waiting for transfers between devices, layer_pass(): lax.psum(second_part, 'mp').reshape(image_total, SIDE * SIDE, C)  108 us
    psum x1, waiting for transfers between devices, layer_pass(): lax.psum(first_part.astype(jnp.bfloat16), 'mp').astype(jnp.float32)  94 us
    psum x1, waiting for transfers between devices, layer_pass(): projected = lax.psum(proj_part, 'mp')  69.2 us
    reduce_scatter x1, waiting for transfers between devices, shards(): lax.psum_scatter(big_totals[0], 'dp', scatter_dimension=0, tiled=True)  62.6 us
    reduce_scatter x1, waiting for transfers between devices, shards(): lax.psum_scatter(big_totals[1], 'dp', scatter_dimension=0, tiled=True)  57 us
    dot_general x20, matrix products, poly_step(): poly = coef_b * gram + coef_c * jnp.dot(gram, gram, precision=highest)  48.7 us
    dot_general x20, matrix products, gram_of(): return jnp.dot(matrix.T, matrix, precision=highest)  44.4 us
  transfers between devices with their start and end apart: 12, of which 11 were waited for; matrix products, arithmetic and copies ran while one was open for 17% of the time, Pallas kernels for 0%

commit v1 on v0

--- a/solution.py
+++ b/solution.py
@@ -12,7 +12,6 @@
 SIDE = 14
 SHIFT = 3
 NS_ITERS = 5
-MB = 2
 IMG_DEV = 16
 TABLE = 169
 
@@ -83,36 +82,38 @@
     ) * (1.0 / math.sqrt(2.0 * math.pi))
 
 
-def gram_of(matrix):
-    return jnp.dot(matrix.T, matrix, precision=highest)
-
-
-def poly_step(matrix, gram):
-    poly = coef_b * gram + coef_c * jnp.dot(gram, gram, precision=highest)
-    return coef_a * matrix + jnp.dot(matrix, poly, precision=highest)
-
-
-def orthogonalize_shared(blocks):
-    iterates = list(blocks)
+def split_low(values):
+    high = lax.reduce_precision(values, exponent_bits=8, mantissa_bits=7)
+    return high.astype(jnp.bfloat16), (values - high).astype(jnp.bfloat16)
+
+
+def dot_three(left, right):
+    left_high, left_rest = left
+    right_high, right_rest = right
+    wide = dict(preferred_element_type=jnp.float32)
+    return (
+        jnp.dot(left_rest, right_high, **wide)
+        + jnp.dot(left_high, right_rest, **wide)
+        + jnp.dot(left_high, right_high, **wide)
+    )
+
+
+def newton_schulz(gram):
+    width = gram.shape[0]
+    eye = jnp.eye(width, dtype=jnp.float32)
+    norm_value = jnp.sqrt(jnp.sum(gram * eye)) + ns_eps
+    gram = gram / (norm_value * norm_value)
+    total = None
     for iteration in range(NS_ITERS):
-        grams = lax.psum(
-            (
-                gram_of(iterates[0]),
-                gram_of(iterates[1]),
-                gram_of(iterates[2]),
-                gram_of(iterates[3]),
-            ),
-            ("dp", "mp"),
-        )
-        grams = list(grams)
-        if iteration == 0:
-            norm_values = [jnp.sqrt(jnp.trace(gram)) + ns_eps for gram in grams]
-            iterates = [matrix / norm_value for matrix, norm_value in zip(iterates, norm_values)]
-            grams = [
-                gram / (norm_value * norm_value) for gram, norm_value in zip(grams, norm_values)
-            ]
-        iterates = [poly_step(matrix, gram) for matrix, gram in zip(iterates, grams)]
-    return tuple(iterates)
+        parts = split_low(gram)
+        square = dot_three(parts, parts)
+        poly = coef_a * eye + (coef_b * gram + coef_c * square)
+        poly_parts = split_low(poly)
+        total = poly if total is None else dot_three(split_low(total), poly_parts)
+        if iteration + 1 < NS_ITERS:
+            half = dot_three(parts, poly_parts)
+            gram = dot_three(split_low(half), poly_parts)
+    return total / norm_value
 
 
 def adam_update(grad_sum, first_moment, second_moment):
@@ -188,7 +189,7 @@
     )
     attended = attended.astype(jnp.bfloat16).reshape(window_count * span, wide)
     proj_part = jnp.dot(attended, proj_local, preferred_element_type=jnp.float32)
-    projected = lax.psum(proj_part, "mp")
+    projected = proj_part
     middle = tokens_in + (
         from_windows(projected.reshape(window_count, span, C), image_total) + vectors[4]
     )
@@ -200,7 +201,7 @@
     )
     acted = gelu_value(hidden).astype(jnp.bfloat16)
     mlp_part = jnp.dot(acted, contract_local, preferred_element_type=jnp.float32)
-    mlp_out = lax.psum(mlp_part.astype(jnp.bfloat16), "mp").astype(jnp.float32)
+    mlp_out = mlp_part
     block_out = middle + (mlp_out.reshape(image_total, SIDE * SIDE, C) + vectors[5])
     block_low = jnp.where(live_block[:, None, None], block_out, 0.0).astype(jnp.bfloat16)
     grad_out = cot_block.astype(jnp.float32) * live_block.astype(jnp.float32)[:, None, None]
@@ -217,7 +218,7 @@
         hidden_grad, second_in, contract_rows, preferred_element_type=jnp.float32
     )
     second_part = jnp.dot(hidden_grad, expand_local, preferred_element_type=jnp.float32)
-    second_grad = lax.psum(second_part, "mp").reshape(image_total, SIDE * SIDE, C)
+    second_grad = second_part.reshape(image_total, SIDE * SIDE, C)
     middle_grad = grad_out + normalize_back(second_grad, normed_two, inv_two, vectors[2])
     attn_low = to_windows(middle_grad.astype(jnp.bfloat16)).reshape(window_count * span, C)
     proj_grad = lax.dot_general(
@@ -264,7 +265,7 @@
         qkv_back, window_in, contract_rows, preferred_element_type=jnp.float32
     )
     first_part = jnp.dot(qkv_back, qkv_local, preferred_element_type=jnp.float32)
-    first_windows = lax.psum(first_part.astype(jnp.bfloat16), "mp").astype(jnp.float32)
+    first_windows = first_part
     first_grad = from_windows(first_windows.reshape(window_count, span, C), image_total)
     input_grad = middle_grad + normalize_back(first_grad, normed_one, inv_one, vectors[0])
     vectors_grad = jnp.stack(
@@ -310,14 +311,25 @@
     pos_index,
     image_counts,
 ):
+    everyone = ("mp", "dp")
     span = WIN * WIN
-    live_all = jnp.arange(IMG_DEV, dtype=jnp.int32) < image_counts[0]
+    mp_size, dp_size = lax.axis_size("mp"), lax.axis_size("dp")
+    mp_index, dp_index = lax.axis_index("mp"), lax.axis_index("dp")
+    devices = mp_size * dp_size
+    per_device = IMG_DEV // mp_size
+    first_image = mp_index * per_device
+    live_all = first_image + jnp.arange(per_device, dtype=jnp.int32) < image_counts[0]
+    own_images = lax.dynamic_slice_in_dim(images, first_image, per_device, 0)
+    own_cotangent = lax.dynamic_slice_in_dim(cotangent, first_image, per_device, 0)
+    qv_full = lax.all_gather(qv_bias, "mp", axis=1, tiled=True)
+    expand_full = lax.all_gather(expand_bias, "mp", axis=0, tiled=True)
+    table_full = lax.all_gather(rel_table, "mp", axis=1, tiled=True)
     onehot = (
         pos_index.reshape(span * span)[:, None] == jnp.arange(TABLE, dtype=jnp.int32)[None, :]
     ).astype(jnp.float32)
-    heads_here = rel_table.shape[1]
+    heads_here = table_full.shape[1]
     pos_bias = (
-        jnp.dot(onehot, rel_table, precision=highest)
+        jnp.dot(onehot, table_full, precision=highest)
         .reshape(span, span, heads_here)
         .transpose(2, 0, 1)
     )
@@ -325,59 +337,85 @@
     window_mask = jnp.where(
         window_regions[:, :, None] != window_regions[:, None, :], mask_value, 0.0
     ).astype(jnp.float32)
-    qkv_shard_low = qkv_weight.astype(jnp.bfloat16)
-    proj_shard_low = proj_weight.astype(jnp.bfloat16)
-    expand_shard_low = expand_weight.astype(jnp.bfloat16)
-    contract_shard_low = contract_weight.astype(jnp.bfloat16)
-    per_batch = IMG_DEV // MB
-    out_blocks = []
-    input_blocks = []
-    for batch_index in range(MB):
-        first_image = batch_index * per_batch
-        gathered = (
-            lax.all_gather(qkv_shard_low, "dp", axis=0, tiled=True),
-            lax.all_gather(proj_shard_low, "dp", axis=0, tiled=True),
-            lax.all_gather(expand_shard_low, "dp", axis=0, tiled=True),
-            lax.all_gather(contract_shard_low, "dp", axis=0, tiled=True),
-        )
-        block_low, input_low, big_local, small_local = layer_pass(
-            images[first_image : first_image + per_batch],
-            cotangent[first_image : first_image + per_batch],
-            live_all[first_image : first_image + per_batch],
-            gathered,
-            vectors,
-            qv_bias,
-            expand_bias,
-            pos_bias,
-            window_mask,
-            onehot,
-        )
-        out_blocks.append(block_low)
-        input_blocks.append(input_low)
-        if batch_index == 0:
-            big_totals = big_local
-            small_totals = small_local
-        else:
-            big_totals = jax.tree.map(jnp.add, big_totals, big_local)
-            small_totals = jax.tree.map(jnp.add, small_totals, small_local)
-    shares = (
-        lax.psum_scatter(big_totals[0], "dp", scatter_dimension=0, tiled=True),
-        lax.psum_scatter(big_totals[1], "dp", scatter_dimension=0, tiled=True),
-        lax.psum_scatter(big_totals[2], "dp", scatter_dimension=0, tiled=True),
-        lax.psum_scatter(big_totals[3], "dp", scatter_dimension=0, tiled=True),
-    )
-    small_sums = lax.psum(
-        (small_totals[0], small_totals[1], small_totals[2], small_totals[3]), "dp"
-    )
     weights_all = (qkv_weight, proj_weight, expand_weight, contract_weight)
     moments = (qkv_moment, proj_moment, expand_moment, contract_moment)
-    buffers = tuple(
-        (muon_beta * moment + grad_share for moment, grad_share in zip(moments, shares))
-    )
-    nesterov = tuple(
-        (grad_share + muon_beta * buffer_new for grad_share, buffer_new in zip(shares, buffers))
-    )
-    ortho = orthogonalize_shared(nesterov)
+    rows = [weight.shape[0] for weight in weights_all]
+    starts = [sum(rows[:which]) for which in range(4)]
+    total_rows = sum(rows)
+
+    def cut(stacked):
+        return [stacked[:, start : start + count] for start, count in zip(starts, rows)]
+
+    own_low = jnp.concatenate(weights_all, axis=0).astype(jnp.bfloat16)
+    gathered = [
+        part.reshape(-1, C) for part in cut(lax.all_gather(own_low, everyone, axis=0, tiled=False))
+    ]
+    block_low, input_low, big_local, small_local = layer_pass(
+        own_images,
+        own_cotangent,
+        live_all,
+        gathered,
+        vectors,
+        qv_full,
+        expand_full,
+        pos_bias,
+        window_mask,
+        onehot,
+    )
+    block_out = lax.all_gather(block_low, "mp", axis=0, tiled=True)
+    input_grad = lax.all_gather(input_low, "mp", axis=0, tiled=True)
+    stacked_grads = jnp.concatenate(
+        [grad.reshape(devices, count, C) for grad, count in zip(big_local, rows)], axis=1
+    ).astype(jnp.bfloat16)
+    own_grads = lax.psum_scatter(
+        stacked_grads.reshape(devices * total_rows, C), everyone, scatter_dimension=0, tiled=True
+    ).astype(jnp.float32)
+    own_moments = jnp.concatenate(moments, axis=0)
+    own_buffers = muon_beta * own_moments + own_grads
+    own_nesterov = own_grads + muon_beta * own_buffers
+    iterate_all = lax.all_gather(
+        own_nesterov.astype(jnp.bfloat16), everyone, axis=0, tiled=False
+    )
+    grams = jnp.stack(
+        [
+            lax.dot_general(
+                part.reshape(-1, C),
+                part.reshape(-1, C),
+                contract_rows,
+                preferred_element_type=jnp.float32,
+            )
+            for part in cut(iterate_all)
+        ]
+    )
+    own_gram = lax.dynamic_index_in_dim(grams, mp_index, 0, keepdims=False)
+    ortho_map = newton_schulz(own_gram)
+    most = max(rows)
+    start_here = jnp.array(starts, jnp.int32)[mp_index]
+    by_group = iterate_all.reshape(mp_size, dp_size, total_rows, C)
+    picked = lax.dynamic_slice(
+        by_group,
+        (jnp.int32(0), dp_index.astype(jnp.int32), start_here, jnp.int32(0)),
+        (mp_size, 1, most, C),
+    ).reshape(mp_size * most, C)
+    map_parts = split_low(ortho_map)
+    products = jnp.dot(picked, map_parts[0], preferred_element_type=jnp.float32) + jnp.dot(
+        picked, map_parts[1], preferred_element_type=jnp.float32
+    )
+    exchanged = lax.all_to_all(products.reshape(mp_size, most, C), "mp", 0, 0, tiled=False)
+    ortho = [exchanged[which, :count] for which, count in enumerate(rows)]
+    shares = [own_grads[start : start + count] for start, count in zip(starts, rows)]
+    buffers = [own_buffers[start : start + count] for start, count in zip(starts, rows)]
+    small_full = lax.psum(small_local, everyone)
+
+    def own_columns(full, width):
+        return lax.dynamic_slice_in_dim(full, mp_index * width, width, full.ndim - 1)
+
+    small_sums = (
+        small_full[0],
+        own_columns(small_full[1], qv_bias.shape[1]),
+        own_columns(small_full[2], expand_bias.shape[0]),
+        own_columns(small_full[3], rel_table.shape[1]),
+    )
     factors = (math.sqrt(3.0), 1.0, math.sqrt(max(1.0, FF / C)), 1.0)
     new_steps = tuple(
         (
@@ -395,8 +433,6 @@
     table_step, table_first_new, table_second_new = adam_update(
         small_sums[3], table_first, table_second
     )
-    block_out = jnp.concatenate(out_blocks, axis=0)
-    input_grad = jnp.concatenate(input_blocks, axis=0)
     return (
         block_out,
         input_grad,

time: 1680 us -> 576 us (0.34)
  waiting for transfers between devices: 985 us -> 165 us
  matrix products: 201 us -> 99.8 us
  blocking collectives: 138 us -> 60.5 us
  other arithmetic: 121 us -> 49.9 us
  local copies, waits for them, and re-layouts: 202 us -> 168 us
    psum x8 -> x0, waiting for transfers between devices: 865 us -> none  [the longest x5 594 us: orthogonalize_shared(): lax.psum((gram_of(iterates[0]), gram_of(iterates[1]), gram_of(iterates[2]...]
    all_gather x0 -> x4, waiting for transfers between devices: none -> 111 us  [the longest x1 64.8 us: shards(): lax.all_gather(own_nesterov.astype(jnp.bfloat16), everyone, axis=0, tiled...]
    all_gather x4 -> x3, blocking collectives: 108 us -> 17 us  [the longest x1 6.11 us: shards(): table_full = lax.all_gather(rel_table, 'mp', axis=1, tiled=True)]
    dot_general x61 -> x58, matrix products: 112 us -> 37.6 us  [the longest x4 11.6 us: shards(): lax.dot_general(part.reshape(-1, C), part.reshape(-1, C), contract_rows,...]
    reduce_scatter x4 -> x1, waiting for transfers between devices: 120 us -> 47.9 us  [shards(): lax.psum_scatter(stacked_grads.reshape(devices * total_rows, C), everyone...]
    convert_element_type x4, local copies, waits for them, and re-layouts: 21 us -> 59.5 us  [layer_pass(): qkv_back = jnp.stack([query_grad, key_grad, value_grad], axis=3).astype(j...]
    reduce_sum x7 -> x1, other arithmetic: 27.3 us -> 1.13 us  [newton_schulz(): norm_value = jnp.sqrt(jnp.sum(gram * eye)) + ns_eps]
    reshape x7 -> x1, local copies, waits for them, and re-layouts: 19.1 us -> 0.21 us  [shards(): pos_bias = jnp.dot(onehot, table_full, precision=highest).reshape(span, s...]
  transfers between devices with their start and end apart: 12 -> 6, of which waited for: 11 -> 5; matrix products, arithmetic and copies ran while one was open for 17% -> 17% of each run, Pallas kernels for 0% -> 0%
where the time goes in v1:
time: 576 us; the launch traced here: 566 us
  local copies, waits for them, and re-layouts  168 us (29%)
  waiting for transfers between devices  165 us (29%)
  matrix products  99.8 us (17%)
  blocking collectives  60.5 us (11%)
  other arithmetic  49.9 us (9%)
  between operations  19.1 us (3%)
    all_gather x1, waiting for transfers between devices, shards(): lax.all_gather(own_nesterov.astype(jnp.bfloat16), everyone, axis=0, tiled...  64.8 us
    convert_element_type x4, local copies, waits for them, and re-layouts, layer_pass(): qkv_back = jnp.stack([query_grad, key_grad, value_grad], axis=3).astype(j...  59.5 us
    reduce_scatter x1, waiting for transfers between devices, shards(): lax.psum_scatter(stacked_grads.reshape(devices * total_rows, C), everyone...  47.9 us
    psum x1, blocking collectives, shards(): small_full = lax.psum(small_local, everyone)  43.5 us
    all_gather x1, waiting for transfers between devices, shards(): lax.all_gather(own_low, everyone, axis=0, tiled=False)  38.1 us
    unnamed x179, local copies, waits for them, and re-layouts  17.5 us
    dot_general x4, matrix products, shards(): lax.dot_general(part.reshape(-1, C), part.reshape(-1, C), contract_rows,...  11.6 us
  transfers between devices with their start and end apart: 6, of which 5 were waited for; matrix products, arithmetic and copies ran while one was open for 17% of the time, Pallas kernels for 0%

profile of v1, /device:TPU:1, one launch (start us, length us, event | category | flops | bytes accessed | tf_op | source)
XLA Modules:
  0.0 566.0 jit_solution(4591520904191398247)
XLA Ops:
  12.1 2.7 constant_dynamic-slice_fusion.3
  24.4 6.1 %all-gather.1 = f32[4,4,169]{2,1,0:T(4,128)S(1)} all-gather(f32[1,4,169]{2,1,0:T(4,128)S(1)} %bitcast.349), channel_id=1, replica_groups=mesh['dp'=8,'mp'=4] {'mp'}, dimensions={0}, use_global_device_ids=true | all-gather | bytes 13520 | tf_op jit(solution)/shard_map/all_gather | solution.py:326
  33.1 5.3 all_gather.26
  38.8 5.7 all-gather.2
  45.2 38.1 %all-gather.8.cloned.1.call-done = bf16[32,192,512]{2,1,0:T(8,128)(2,1)} async-done(((bf16[1,192,512]{2,1,0:T(8,128)(2,1)}), bf16[32,192,512]{2,1,0:T(8,128)(2,1)}) %all-gather.8.cloned.1.call-update) | async-done | bytes 6291472 | tf_op jit(solution)/shard_map/all_gather | solution.py:351
  83.4 1.5 slice.230
  86.0 2.9 add_convert_fusion
  88.9 3.4 copy.158
  92.3 11.0 %reshape.334 = bf16[16,49,16,3,32]{1,0,4,3,2:T(8,128)(2,1)} reshape(bf16[784,1536]{0,1:T(8,128)(2,1)S(1)} %copy.158) | data formatting | bytes 4816896 | tf_op jit(solution)/shard_map/reshape | solution.py:161
  103.4 4.5 fusion.184
  107.9 3.2 fusion.189
  111.1 2.3 fusion
  114.0 2.3 convert_bitcast_fusion
  116.3 3.9 copy.198
  120.3 5.7 %reshape.372 = bf16[4,2,2,7,7,512]{5,4,3,2,1,0:T(8,128)(2,1)} reshape(bf16[16,49,16,32]{3,2,1,0:T(8,128)(2,1)} %copy.198) | data formatting | bytes 1605632 | tf_op jit(solution)/shard_map/dot_general | solution.py:191
  127.9 2.0 convolution_bitcast_fusion
  129.8 1.3 copy.167
  133.8 2.7 fusion.183
  136.6 1.9 fusion.193
  138.6 8.0 %convert_reduce_fusion.2 = (f32[2048]{0:T(1024)}, bf16[784,2048]{1,0:T(8,128)(2,1)}, bf16[784,2048]{1,0:T(8,128)(2,1)}, f32[784,2048]{1,0:T(8,128)}) fusion(f32[784,2048]{1,0:T(8,128)S(1)} %fusion.193, f32[2048]{0:T(1024)S(1)} %bitcast.328, bf16[784,512]{1,0:T(8,128)(2,1)S(1)} %copy-done.36, bf16[2048,512]{1,0:T(8,128)(2,1)S(1)} %bitcast.313), kind=kOutput, calls=%fused_computation.30 | convolution fusion | flops 1669855232 | bytes 22183936 | tf_op jit(solution)/shard_map/dot_general | solution.py:212
  146.6 3.4 dot_general.262
  150.0 5.6 multiply_reduce_fusion.1
  155.6 1.7 fusion.178
  161.4 2.9 reshape.378
  164.4 5.4 copy.173
  169.8 7.3 %fusion.24 = bf16[16,49,16,1,32]{1,4,2,0,3:T(8,128)(2,1)} fusion(bf16[16,49,16,32]{1,3,2,0:T(8,128)(2,1)} %copy.173, f32[16,16,49,49]{2,3,1,0:T(8,128)} %copy-done, f32[16,16,49]{2,1,0:T(8,128)S(1)} %log_add_fusion), kind=kOutput, calls=%fused_computation.56 | convolution fusion | flops 40567296 | bytes 4114432 | tf_op jit(solution)/shard_map/whij,wihd->wjhd/dot_general | solution.py:232
  177.1 2.5 multiply_reduce_fusion
  179.7 3.4 convert_reduce_fusion.1
  183.1 3.3 multiply_bitcast_fusion
  186.4 2.9 multiply_bitcast_fusion.1
  190.4 2.8 copy.185
  194.4 8.5 %fusion.12 = (bf16[2048,784]{0,1:T(8,128)(2,1)S(1)}, bf16[2048,784]{0,1:T(8,128)(2,1)}) fusion(f32[784,2048]{1,0:T(8,128)} %get-tuple-element.224, f32[784,2048]{1,0:T(8,128)} %copy-done.24, f32[2048]{0:T(1024)S(1)} %bitcast.329), kind=kLoop, calls=%fused_computation.23 | loop fusion | flops 22478848 | bytes 19275776 | tf_op jit(solution)/shard_map/convert_element_type | solution.py:215
  202.9 6.0 %copy.187 = bf16[2048,784]{1,0:T(8,128)(2,1)} copy(bf16[2048,784]{0,1:T(8,128)(2,1)} %get-tuple-element.196) | data formatting | bytes 6422528 | tf_op jit(solution)/shard_map/convert_element_type | solution.py:202
  208.9 4.0 copy.186
  212.9 4.6 reshape.349
  217.5 5.1 convert_reduce_fusion
  222.6 2.6 copy-done.1
  225.2 10.0 %copy.184 = bf16[16,49,16,3,32]{1,0,4,3,2:T(8,128)(2,1)} copy(bf16[16,49,16,3,32]{1,4,2,0,3:T(8,128)(2,1)S(1)} %get-tuple-element.184) | data formatting | bytes 4816896 | tf_op jit(solution)/shard_map/convert_element_type | solution.py:259
  235.2 9.6 %convert_element_type.257 = bf16[784,1536]{0,1:T(8,128)(2,1)S(1)} reshape(bf16[16,49,16,3,32]{1,0,4,3,2:T(8,128)(2,1)} %copy.184) | data formatting | bytes 4816896 | tf_op jit(solution)/shard_map/convert_element_type | solution.py:259
  244.9 4.5 convolution_convert_fusion
  249.4 2.4 convolution_convert_fusion.1
  253.0 1.8 convolution_convert_fusion.2
  254.8 3.3 pad_maximum_fusion
  258.1 3.6 dot_general.259
  261.8 5.5 select_convert_fusion
  267.3 20.7 %copy.199 = bf16[16,49,16,3,32]{4,3,2,1,0:T(4,128)(2,1)} copy(bf16[16,49,16,3,32]{1,4,2,0,3:T(8,128)(2,1)} %copy-done.1) | data formatting | bytes 4816896 | tf_op jit(solution)/shard_map/convert_element_type | solution.py:259
  288.0 19.2 %reshape.373 = bf16[4,2,2,7,7,1536]{5,4,3,2,1,0:T(8,128)(2,1)S(1)} reshape(bf16[16,49,16,3,32]{4,3,2,1,0:T(4,128)(2,1)} %copy.199) | data formatting | bytes 4816896 | tf_op jit(solution)/shard_map/convert_element_type | solution.py:259
  307.3 3.9 convolution_bitcast_fusion.1
  313.5 1.6 multiply_reduce_fusion.4
  315.5 2.5 fusion.45
  318.1 3.2 fusion.44
  321.6 47.9 %reduce-scatter.2.cloned.1.call-done = bf16[192,512]{1,0:T(8,128)(2,1)} async-done(((bf16[6144,512]{1,0:T(8,128)(2,1)}), bf16[192,512]{1,0:T(8,128)(2,1)}) %reduce-scatter.2.cloned.1.call-update) | async-done | bytes 196624 | tf_op jit(solution)/shard_map/reduce_scatter | solution.py:370
  369.5 1.7 fusion.123
  375.4 43.5 %all-reduce = (f32[6,512]{1,0:T(8,128)S(1)}, f32[2,512]{1,0:T(2,128)S(1)}, f32[2048]{0:T(1024)S(1)}, f32[169,16]{0,1:T(8,128)S(1)}) all-reduce(f32[6,512]{1,0:T(8,128)S(1)} %stack.62, f32[2,512]{1,0:T(2,128)S(1)} %pad_maximum_fusion.10, f32[2048]{0:T(1024)S(1)} %copy-done.69, ...), channel_id=1, replica_groups=mesh['dp'=8,'mp'=4] {'mp','dp'}, use_global_device_ids=true, to_apply=%region_19.20 | all-reduce | flops 8848 | bytes 70784 | tf_op jit(solution)/shard_map/psum | solution.py:408
  421.5 4.7 copy.190
  426.1 7.8 %all-gather.12.cloned.1.call-done = bf16[16,196,512]{2,1,0:T(8,128)(2,1)} async-done(((bf16[4,196,512]{2,1,0:T(8,128)(2,1)}), bf16[16,196,512]{2,1,0:T(8,128)(2,1)}) %all-gather.12.cloned.1.call-update) | async-done | bytes 3211280 | tf_op jit(solution)/shard_map/all_gather | solution.py:366
  433.9 4.7 copy.191
  441.1 64.8 %all-gather.14.cloned.1.call-done = bf16[6144,512]{1,0:T(8,128)(2,1)} async-done(((bf16[192,512]{1,0:T(8,128)(2,1)}), bf16[6144,512]{1,0:T(8,128)(2,1)}) %all-gather.14.cloned.1.call-update) | async-done | bytes 6291472 | tf_op jit(solution)/shard_map/all_gather | solution.py:376
  505.9 3.5 fusion.58
  509.4 3.5 fusion.55
  512.9 1.8 convolution_bitcast_fusion.2
  514.7 2.9 fusion.52
  545.5 3.7 all-to-all-start
  550.6 6.4 %all-to-all-done = f32[4,64,512]{2,1,0:T(8,128)S(1)} async-done(((f32[4,64,512]{2,1,0:T(8,128)}), f32[4,64,512]{2,1,0:T(8,128)S(1)}, u32[]{:S(2)}, u32[]{:S(2)}) %all-to-all-start) | async-done | bytes 524320 | tf_op jit(solution)/shard_map/all_to_all | solution.py:404
  (342 shorter events, 71.6 us)
Async XLA Ops:
  7.2 76.2 %all-gather.8.cloned.1.call-start = ((), (), s32[]{:S(2)}) async-start(), calls=%async_computation.2 | async-start | bytes 6488064 | tf_op jit(solution)/shard_map/all_gather | solution.py:351
  10.6 358.9 %reduce-scatter.2.cloned.1.call-start = ((), (), s32[]{:S(2)}) async-start(), calls=%async_computation.5 | async-start | bytes 6488064 | tf_op jit(solution)/shard_map/reduce_scatter | solution.py:370
  12.1 3.5 copy-start.64
  14.8 4.2 copy-start.22
  14.8 117.0 %copy-start.2 = (bf16[4,196,512]{2,0,1:T(4,128)(2,1)}, bf16[4,196,512]{2,0,1:T(4,128)(2,1)S(1)}, u32[]{:S(2)}) copy-start(bf16[4,196,512]{2,0,1:T(4,128)(2,1)S(1)} %get-tuple-element.243) | copy-start | bytes 2408452
  22.6 7.9 %copy-start.57 = (s32[49,49]{1,0:T(8,128)S(1)}, s32[49,49]{1,0:T(8,128)}, u32[]{:S(2)}) copy-start(s32[49,49]{1,0:T(8,128)} %param.49) | copy-start | bytes 28816
  22.8 10.3 %copy-start.81 = (f32[2,128]{1,0:T(2,128)S(1)}, f32[2,128]{1,0:T(2,128)}, u32[]{:S(2)}) copy-start(f32[2,128]{1,0:T(2,128)} %param.37) | copy-start | bytes 3076
  22.9 16.0 %copy-start.77 = (f32[512]{0:T(512)S(1)}, f32[512]{0:T(512)}, u32[]{:S(2)}) copy-start(f32[512]{0:T(512)} %param.38) | copy-start | bytes 6148
  30.6 54.2 %copy-start.62 = (s32[2401]{0:T(1024)}, s32[2401]{0:T(1024)S(1)}, u32[]{:S(2)}) copy-start(s32[2401]{0:T(1024)S(1)} %eq.28) | copy-start | bytes 28816
  103.3 4.5 copy-start.42
  103.4 4.5 copy-start.31
  107.8 3.2 copy-start.7
  107.8 3.2 copy-start.9
  107.8 5.6 copy-start.13
  116.3 3.9 copy-start.15
  132.9 22.7 %copy-start.4 = (f32[4,196,512]{2,1,0:T(8,128)}, f32[4,196,512]{2,1,0:T(8,128)S(1)}, u32[]{:S(2)}) copy-start(f32[4,196,512]{2,1,0:T(8,128)S(1)} %get-tuple-element.194) | copy-start | bytes 4816900
  138.5 8.1 %copy-start.24 = (f32[784,2048]{1,0:T(8,128)}, f32[784,2048]{1,0:T(8,128)S(1)}, u32[]{:S(2)}) copy-start(f32[784,2048]{1,0:T(8,128)S(1)} %fusion.193) | copy-start | bytes 19267588
  150.0 5.6 copy-start.23
  150.0 5.6 copy-start.71
  164.4 12.7 %slice-start = ((s8[7340032]{0:T(1024)(128)(4,1)}), s8[3145728]{0:T(1024)(128)(4,1)S(1)}, s32[]{:S(2)}) async-start(s8[7340032]{0:T(1024)(128)(4,1)} %bitcast.290), calls=%async_computation.7 | async-start | bytes 6291456
  169.8 7.3 %slice-start.1 = ((s8[7340032]{0:T(1024)(128)(4,1)}), s8[4194304]{0:T(1024)(128)(4,1)S(1)}, s32[]{:S(2)}) async-start(s8[7340032]{0:T(1024)(128)(4,1)} %bitcast.290), calls=%async_computation.8 | async-start | bytes 8388608
  169.8 7.3 %copy-start.6 = (bf16[16,49,16,32]{1,3,2,0:T(8,128)(2,1)S(1)}, bf16[16,49,16,32]{1,3,2,0:T(8,128)(2,1)}, u32[]{:S(2)}) copy-start(bf16[16,49,16,32]{1,3,2,0:T(8,128)(2,1)} %copy.173) | copy-start | bytes 2408452
  169.8 7.3 %copy-start.14 = (bf16[16,49,16,1,32]{1,0,4,3,2:T(8,128)(2,1)S(1)}, bf16[16,49,16,1,32]{1,0,4,3,2:T(8,128)(2,1)}, u32[]{:S(2)}) copy-start(bf16[16,49,16,1,32]{1,0,4,3,2:T(8,128)(2,1)} %copy-done.13) | copy-start | bytes 2408452
  179.6 3.4 copy-start.10
  183.1 3.3 copy-start.8
  186.4 4.0 copy-start.16
  212.9 4.6 copy-start.17
  235.2 9.6 %copy-start.35 = (bf16[784,512,1]{1,0,2:T(8,128)(2,1)S(1)}, bf16[784,512,1]{1,0,2:T(8,128)(2,1)}, u32[]{:S(2)}) copy-start(bf16[784,512,1]{1,0,2:T(8,128)(2,1)} %reshape.367) | copy-start | bytes 2408452
  244.8 4.6 copy-start.25
  244.8 4.6 copy-start.37
  258.1 163.4 %all-gather.10.cloned.1.call-start = ((), (), s32[]{:S(2)}) async-start(), calls=%async_computation.3 | async-start | bytes 4096000 | tf_op jit(solution)/shard_map/all_gather | solution.py:365
  258.1 3.7 copy-start.5
  258.1 3.7 copy-start.78
  258.1 3.6 copy-start.84
  267.3 166.7 %all-gather.12.cloned.1.call-start = ((), (), s32[]{:S(2)}) async-start(), calls=%async_computation.4 | async-start | bytes 4096000 | tf_op jit(solution)/shard_map/all_gather | solution.py:366
  318.0 51.5 %copy-start.44 = (f32[64,512]{1,0:T(8,128)S(1)}, f32[64,512]{1,0:T(8,128)}, u32[]{:S(2)}) copy-start(f32[64,512]{1,0:T(8,128)} %param.35) | copy-start | bytes 393220
  318.1 51.4 %copy-start.45 = (f32[64,512]{1,0:T(8,128)S(1)}, f32[64,512]{1,0:T(8,128)}, u32[]{:S(2)}) copy-start(f32[64,512]{1,0:T(8,128)} %param.34) | copy-start | bytes 393220
  318.1 51.4 %copy-start.49 = (f32[48,512]{1,0:T(8,128)S(1)}, f32[48,512]{1,0:T(8,128)}, u32[]{:S(2)}) copy-start(f32[48,512]{1,0:T(8,128)} %param.32) | copy-start | bytes 294916
  318.1 51.4 %copy-start.56 = (f32[16,512]{1,0:T(8,128)S(1)}, f32[16,512]{1,0:T(8,128)}, u32[]{:S(2)}) copy-start(f32[16,512]{1,0:T(8,128)} %param.33) | copy-start | bytes 98308
  321.3 49.9 %copy-start.85 = (s32[4]{0:T(128)S(1)}, s32[4]{0:T(128)}, u32[]{:S(2)}) copy-start(s32[4]{0:T(128)} %constant.31.clone) | copy-start | bytes 52
  321.3 52.4 %copy-start.50 = (f32[16,3,32]{2,0,1:T(8,128)S(1)}, f32[16,3,32]{2,0,1:T(8,128)}, u32[]{:S(2)}) copy-start(f32[16,3,32]{2,0,1:T(8,128)} %get-tuple-element.183) | copy-start | bytes 18436
  321.3 52.6 %copy-start.30 = (f32[16,49,49]{1,2,0:T(8,128)S(1)}, f32[16,49,49]{1,2,0:T(8,128)}, u32[]{:S(2)}) copy-start(f32[16,49,49]{1,2,0:T(8,128)} %get-tuple-element.179) | copy-start | bytes 460996
  321.3 53.1 %copy-start.65 = (f32[512]{0:T(512)S(1)}, f32[512]{0:T(512)}, u32[]{:S(2)}) copy-start(f32[512]{0:T(512)} %get-tuple-element.185) | copy-start | bytes 6148
  321.3 53.1 %copy-start.66 = (f32[512]{0:T(512)S(1)}, f32[512]{0:T(512)}, u32[]{:S(2)}) copy-start(f32[512]{0:T(512)} %get-tuple-element.205) | copy-start | bytes 6148
  321.4 53.1 %copy-start.75 = (f32[512]{0:T(512)S(1)}, f32[512]{0:T(512)}, u32[]{:S(2)}) copy-start(f32[512]{0:T(512)} %get-tuple-element.150) | copy-start | bytes 6148
  321.4 53.1 %copy-start.76 = (f32[512]{0:T(512)S(1)}, f32[512]{0:T(512)}, u32[]{:S(2)}) copy-start(f32[512]{0:T(512)} %get-tuple-element.155) | copy-start | bytes 6148
  321.4 53.1 %copy-start.63 = (s32[2401]{0:T(1024)S(1)}, s32[2401]{0:T(1024)}, u32[]{:S(2)}) copy-start(s32[2401]{0:T(1024)} %copy-done.62) | copy-start | bytes 28816
  321.4 54.0 %copy-start.69 = (f32[2048]{0:T(1024)S(1)}, f32[2048]{0:T(1024)}, u32[]{:S(2)}) copy-start(f32[2048]{0:T(1024)} %get-tuple-element.181) | copy-start | bytes 24580
  321.4 97.5 %copy-start.82 = (f32[2,128]{1,0:T(2,128)S(1)}, f32[2,128]{1,0:T(2,128)}, u32[]{:S(2)}) copy-start(f32[2,128]{1,0:T(2,128)} %param.42) | copy-start | bytes 3076
  321.4 97.5 %copy-start.83 = (f32[2,128]{1,0:T(2,128)S(1)}, f32[2,128]{1,0:T(2,128)}, u32[]{:S(2)}) copy-start(f32[2,128]{1,0:T(2,128)} %param.43) | copy-start | bytes 3076
  321.5 98.1 %copy-start.79 = (f32[512]{0:T(512)S(1)}, f32[512]{0:T(512)}, u32[]{:S(2)}) copy-start(f32[512]{0:T(512)} %param.44) | copy-start | bytes 6148
  321.5 98.1 %copy-start.80 = (f32[512]{0:T(512)S(1)}, f32[512]{0:T(512)}, u32[]{:S(2)}) copy-start(f32[512]{0:T(512)} %param.45) | copy-start | bytes 6148
  321.5 98.7 %copy-start.73 = (f32[169,4]{0,1:T(4,128)S(1)}, f32[169,4]{0,1:T(4,128)}, u32[]{:S(2)}) copy-start(f32[169,4]{0,1:T(4,128)} %param.46) | copy-start | bytes 8116
  321.5 98.7 %copy-start.74 = (f32[169,4]{0,1:T(4,128)S(1)}, f32[169,4]{0,1:T(4,128)}, u32[]{:S(2)}) copy-start(f32[169,4]{0,1:T(4,128)} %param.47) | copy-start | bytes 8116
  321.5 99.3 %copy-start.59 = (f32[6,512]{1,0:T(8,128)S(1)}, f32[6,512]{1,0:T(8,128)}, u32[]{:S(2)}) copy-start(f32[6,512]{1,0:T(8,128)} %param.40) | copy-start | bytes 36868
  321.5 99.3 %copy-start.60 = (f32[6,512]{1,0:T(8,128)S(1)}, f32[6,512]{1,0:T(8,128)}, u32[]{:S(2)}) copy-start(f32[6,512]{1,0:T(8,128)} %param.41) | copy-start | bytes 36868
  321.5 184.4 %all-gather.14.cloned.1.call-start = ((), (), s32[]{:S(2)}) async-start(), calls=%async_computation.6 | async-start | bytes 6488064 | tf_op jit(solution)/shard_map/all_gather | solution.py:376
  418.9 7.2 %copy-start.61 = (f32[6,512]{1,0:T(8,128)}, f32[6,512]{1,0:T(8,128)S(1)}, u32[]{:S(2)}) copy-start(f32[6,512]{1,0:T(8,128)S(1)} %get-tuple-element.158) | copy-start | bytes 36868
  426.1 13.7 %copy-start.32 = (bf16[192,512]{1,0:T(8,128)(2,1)S(1)}, bf16[192,512]{1,0:T(8,128)(2,1)}, u32[]{:S(2)}) copy-start(bf16[192,512]{1,0:T(8,128)(2,1)} %reduce-scatter.2.cloned.1.call-done) | copy-start | bytes 589828
  544.3 12.7 %copy-start.43 = (f32[48,512]{1,0:T(8,128)S(1)}, f32[48,512]{1,0:T(8,128)}, u32[]{:S(2)}) copy-start(f32[48,512]{1,0:T(8,128)} %param.28) | copy-start | bytes 294916
  544.3 13.4 %copy-start.46 = (f32[16,512]{1,0:T(8,128)S(1)}, f32[16,512]{1,0:T(8,128)}, u32[]{:S(2)}) copy-start(f32[16,512]{1,0:T(8,128)} %param.29) | copy-start | bytes 98308
  544.3 14.0 %copy-start.40 = (f32[64,512]{1,0:T(8,128)S(1)}, f32[64,512]{1,0:T(8,128)}, u32[]{:S(2)}) copy-start(f32[64,512]{1,0:T(8,128)} %param.31) | copy-start | bytes 393220
  544.3 14.0 %copy-start.41 = (f32[64,512]{1,0:T(8,128)S(1)}, f32[64,512]{1,0:T(8,128)}, u32[]{:S(2)}) copy-start(f32[64,512]{1,0:T(8,128)} %param.30) | copy-start | bytes 393220
  545.5 11.5 %all-to-all-start = ((f32[4,64,512]{2,1,0:T(8,128)}), f32[4,64,512]{2,1,0:T(8,128)S(1)}, u32[]{:S(2)}, u32[]{:S(2)}) async-start(f32[4,64,512]{2,1,0:T(8,128)} %bitcast.84), calls=%async_computation.1 | async-start | bytes 1048576 | tf_op jit(solution)/shard_map/all_to_all | solution.py:404
  (30 other events, 53.2 us)
Sparse Core Ops, SparseCore 0:
  11.6 71.7 all-gather.7
  258.2 111.2 reduce-scatter.1
  371.6 31.1 all-gather.9
  404.3 29.5 all-gather.11
  436.7 69.1 all-gather.13
